TPU v7x, 32 devices: a whole 2x2x4 slice. The times are simulated.
32 devices in a mesh: dp: 4 (over x, core), pipe: 8 (over z, y).
Axes of the slice: x: 2, y: 2, z: 4, core: 2. Of those that a mesh axis runs over, the one named last changes fastest.
Arguments:
- pre: bfloat16 [512, 49152], P('dp', 'pipe'), may hold values from -6 to 6
- grad_out: bfloat16 [512, 6144], P('dp', 'pipe'), may hold values from -6 to 6
- weight_slots: bfloat16 [8, 292, 128, 128], P('pipe', 'dp'), may hold values from -0.21875 to 0.21875
- block_rows: int32 [8, 292], P('pipe', 'dp'), may hold values from 0 to 47, as said below
- block_cols: int32 [8, 292], P('pipe', 'dp'), may hold values from 0 to 47, as said below
- block_count: int32 [8, 4], P('pipe', 'dp'), may hold values from 0 to 73, as said below
Outputs:
- pre_grad: bfloat16 [512, 49152], P('dp', 'pipe')
- weight_grad: bfloat16 [8, 292, 128, 128], P('pipe', 'dp')
Inputs may be any that keep to these rules, and one draw needn't show every extreme that they name: `block_rows`: live slots of slab p list each of its 48 rows of blocks exactly 6 times, with distinct columns; dead slots hold valid indices. `block_cols`: within a row of blocks the live columns are distinct. `block_count`: the counts of one slab sum to 288; in every slab some device holds exactly 73.
All inputs are finite; a program needn't handle non-finite values.
Results may differ from a plain program's by a relative error of at most 0.009.
Values may be sent and summed in bfloat16 or wider, within the bound.
A program may use at most 128 MiB of HBM per device.

v0:
```python
import jax
import jax.numpy as jnp
from jax import lax
from jax.sharding import PartitionSpec as P

BLOCK = 128
inv_root_two = 0.7071067811865476
inverse_square_root_tau = 0.3989422804014327


def gelu_parts(pre_wide):
    normal_cdf = 0.5 * (1.0 + jax.scipy.special.erf(pre_wide * inv_root_two))
    density = jnp.exp(-0.5 * pre_wide * pre_wide) * inverse_square_root_tau
    return (pre_wide * normal_cdf, normal_cdf + pre_wide * density)


def on_device(pre, grad_out, weight_slots, block_rows, block_cols, block_count):
    tok_rows = pre.shape[0]
    slab_rows = pre.shape[1] // BLOCK
    slot_cap = weight_slots.shape[1]
    whole_grad = lax.all_gather(grad_out, "pipe", axis=1, tiled=True)
    grad_blocks = whole_grad.reshape(tok_rows, -1, BLOCK)
    pre_wide = pre.astype(jnp.float32)
    activation, slopes = gelu_parts(pre_wide)
    activation = activation.astype(jnp.bfloat16)
    act_blocks = activation.reshape(tok_rows, slab_rows, BLOCK)
    row_range = jnp.arange(slab_rows)
    all_rows, all_cols, all_counts = (
        lax.all_gather(block_rows, "dp", axis=1, tiled=True),
        lax.all_gather(block_cols, "dp", axis=1, tiled=True),
        lax.all_gather(block_count, "dp", axis=1, tiled=True),
    )
    live_all = jnp.arange(all_rows.shape[1]) % slot_cap < jnp.repeat(all_counts[0], slot_cap)
    row_ids = all_rows[0]
    col_ids = all_cols[0]
    live_mask = live_all
    gradient_fragments = grad_blocks[:, col_ids, :]
    masked = (
        lax.all_gather(weight_slots, "dp", axis=1, tiled=True)[0]
        * live_mask.astype(jnp.bfloat16)[:, None, None]
    )
    value_portion = jnp.einsum(
        "tkd,khd->tkh", gradient_fragments, masked, preferred_element_type=jnp.float32
    )
    row_hot = (row_ids[:, None] == row_range[None, :]).astype(jnp.float32)
    hidden_grad = jnp.einsum("tkh,kr->trh", value_portion, row_hot)
    row_ids = all_rows[0]
    col_ids = all_cols[0]
    live_mask = live_all
    act_pieces = act_blocks[:, row_ids, :]
    gradient_fragments = grad_blocks[:, col_ids, :]
    grad_term = jnp.einsum(
        "tkh,tkd->khd", act_pieces, gradient_fragments, preferred_element_type=jnp.float32
    )
    own_grad = lax.psum_scatter(
        (grad_term * live_mask.astype(jnp.float32)[:, None, None]).astype(jnp.bfloat16),
        "dp",
        scatter_dimension=0,
        tiled=True,
    )
    weight_grad = own_grad[None]
    pre_grad = (hidden_grad.reshape(tok_rows, -1) * slopes).astype(jnp.bfloat16)
    return (pre_grad, weight_grad)


def solution(mesh):
    in_specs = (
        P("dp", "pipe"),
        P("dp", "pipe"),
        P("pipe", "dp", None, None),
        P("pipe", "dp"),
        P("pipe", "dp"),
        P("pipe", "dp"),
    )
    out_specs = (P("dp", "pipe"), P("pipe", "dp", None, None))
    return jax.shard_map(
        on_device, mesh=mesh, in_specs=in_specs, out_specs=out_specs, check_vma=False
    )
```

profile of v0, /device:TPU:0, one launch (start us, length us, event | category | flops | bytes accessed | tf_op | source)
XLA Modules:
  0.0 271.9 jit_solution(10886016366637159782)
XLA Ops:
  7.2 0.0 copy-start.1
  7.2 0.0 all-gather.5.cloned.1.call-start
  7.2 1.9 copy.18
  9.1 0.0 all-gather.5.cloned.1.call-update
  9.1 0.0 all-gather.3.cloned.1.call-start
  9.1 0.7 all-gather.3.cloned.1.call-update
  9.8 0.0 reduce-scatter.2.cloned.1.call-start
  10.5 1.2 dynamic-slice
  12.4 0.7 bitcast_dynamic-update-slice_fusion.1
  13.1 0.8 bitcast_dynamic-update-slice_fusion
  13.9 0.7 bitcast_dynamic-update-slice_fusion.2
  14.6 6.4 %all-reduce.3 = (s32[292]{0:T(512)S(1)}, s32[4]{0:T(128)S(1)}, s32[292]{0:T(512)S(1)}) all-reduce(s32[292]{0:T(512)S(1)} %bitcast_dynamic-update-slice_fusion, s32[4]{0:T(128)S(1)} %bitcast_dynamic-update-slice_fusion.1, s32[292]{0:T(512)S(1)} %bitcast_dynamic-update-slice_fusion.2), channel_id=1, replica_groups=mesh['dp'=4,'pipe'=8] {'dp'}, use_global_device_ids=true, to_apply=%add.2 | all-reduce | flops 588 | bytes 4704
  21.1 0.1 broadcast_in_dim.4
  21.1 0.1 reshape.94
  21.3 0.0 copy-done.1
  21.3 1.6 copy.21
  22.9 34.8 %all-gather.5.cloned.1.call-done = bf16[128,6144]{0,1:T(8,128)(2,1)} async-done(((bf16[128,768]{0,1:T(8,128)(2,1)}), bf16[128,6144]{0,1:T(8,128)(2,1)}) %all-gather.5.cloned.1.call-update) | async-done | bytes 1572880 | tf_op jit(solution)/shard_map/all_gather | solution.py:21
  57.7 1.9 copy.19
  59.6 11.1 %gather_fusion = bf16[292,128,128]{2,1,0:T(8,128)(2,1)} fusion(bf16[128,48,128]{2,0,1:T(8,128)(2,1)S(1)} %copy.19, s32[1024]{0:T(1024)S(1)} %pad_clamp_fusion.1), kind=kCustom, calls=%fused_computation | custom fusion | bytes 19137680 | tf_op jit(solution)/shard_map/gather | solution.py:37
  70.7 51.8 %all-gather.3.cloned.1.call-done = bf16[1,292,128,128]{3,2,0,1:T(8,128)(2,1)} async-done(((bf16[1,73,128,128]{3,2,0,1:T(8,128)(2,1)}), bf16[1,292,128,128]{3,2,0,1:T(8,128)(2,1)}) %all-gather.3.cloned.1.call-update) | async-done | bytes 9568272 | tf_op jit(solution)/shard_map/all_gather | solution.py:39
  122.6 12.9 %fusion.5 = bf16[128,292,128]{0,2,1:T(8,128)(2,1)} fusion(bf16[292,128,128]{2,1,0:T(8,128)(2,1)} %gather_fusion, bf16[1,292,128,128]{3,2,0,1:T(8,128)(2,1)} %all-gather.3.cloned.1.call-done, bf16[292]{0:T(512)(128)(2,1)S(1)} %convert_element_type.27), kind=kOutput, calls=%fused_computation.9 | convolution fusion | flops 1229520896 | bytes 28705352 | tf_op jit(solution)/shard_map/tkd,khd->tkh/dot_general | solution.py:42
  135.5 13.7 %copy.20 = bf16[128,292,128]{2,1,0:T(8,128)(2,1)} copy(bf16[128,292,128]{0,2,1:T(8,128)(2,1)} %fusion.5) | data formatting | bytes 19136512 | tf_op jit(solution)/shard_map/tkd,khd->tkh/transpose | solution.py:42
  149.2 7.5 %convolution_bitcast_fusion = f32[128,48,128]{2,1,0:T(8,128)} fusion(bf16[128,292,128]{2,1,0:T(8,128)(2,1)} %copy.20, s32[292]{0:T(512)S(1)} %get-tuple-element.8), kind=kOutput, calls=%fused_computation.25 | convolution fusion | flops 459290304 | bytes 12715152 | tf_op jit(solution)/shard_map/tkh,kr->trh/dot_general | solution.py:46
  156.6 2.4 copy.27
  159.1 4.0 %fusion.21 = (bf16[128,6144]{0,1:T(8,128)(2,1)}, bf16[128,6144]{0,1:T(8,128)(2,1)}) fusion(bf16[128,6144]{0,1:T(8,128)(2,1)} %copy.21, f32[128,48,128]{0,2,1:T(8,128)S(1)} %copy.27), kind=kLoop, calls=%fused_computation.24 | loop fusion | flops 10223616 | bytes 7864320 | tf_op jit(solution)/shard_map/convert_element_type | solution.py:25
  163.0 1.9 copy.23
  164.9 10.5 %gather_fusion.1 = bf16[292,128,128]{2,1,0:T(8,128)(2,1)} fusion(bf16[128,48,128]{2,0,1:T(8,128)(2,1)S(1)} %copy.23, s32[1024]{0:T(1024)S(1)} %pad_clamp_fusion), kind=kCustom, calls=%fused_computation.1 | custom fusion | bytes 19137680 | tf_op jit(solution)/shard_map/gather | solution.py:50
  175.4 11.1 %multiply_convert_fusion = bf16[292,128,128]{2,1,0:T(8,128)(2,1)} fusion(f32[292]{0:T(512)S(1)} %get-tuple-element.9, bf16[292,128,128]{2,1,0:T(8,128)(2,1)} %gather_fusion, bf16[292,128,128]{2,1,0:T(8,128)(2,1)} %gather_fusion.1), kind=kOutput, calls=%fused_computation.2 | convolution fusion | flops 1234305024 | bytes 28705936 | tf_op jit(solution)/shard_map/tkh,tkd->khd/dot_general | solution.py:52
  186.5 0.0 reduce-scatter.2.cloned.1.call-update
  186.5 1.4 copy-done
  187.9 1.6 copy.25
  189.4 76.0 %reduce-scatter.2.cloned.1.call-done = bf16[73,128,128]{2,1,0:T(8,128)(2,1)} async-done(((bf16[292,128,128]{2,1,0:T(8,128)(2,1)}), bf16[73,128,128]{2,1,0:T(8,128)(2,1)}) %reduce-scatter.2.cloned.1.call-update) | async-done | bytes 2392080 | tf_op jit(solution)/shard_map/reduce_scatter | solution.py:55
  (10 shorter events, 0.1 us)
Async XLA Ops:
  7.2 14.1 %copy-start.1 = (bf16[128,6144]{1,0:T(8,128)(2,1)S(1)}, bf16[128,6144]{1,0:T(8,128)(2,1)}, u32[]{:S(2)}) copy-start(bf16[128,6144]{1,0:T(8,128)(2,1)} %param.6) | copy-start | bytes 4718596
  7.2 50.5 %all-gather.5.cloned.1.call-start = ((), (), s32[]{:S(2)}) async-start(), calls=%async_computation.2 | async-start | bytes 1769472 | tf_op jit(solution)/shard_map/all_gather | solution.py:21
  9.1 113.5 %all-gather.3.cloned.1.call-start = ((), (), s32[]{:S(2)}) async-start(), calls=%async_computation.1 | async-start | bytes 11960320 | tf_op jit(solution)/shard_map/all_gather | solution.py:39
  9.8 255.6 %reduce-scatter.2.cloned.1.call-start = ((), (), s32[]{:S(2)}) async-start(), calls=%async_computation.3 | async-start | bytes 11960320 | tf_op jit(solution)/shard_map/reduce_scatter | solution.py:55
  186.5 1.4 copy-start
Sparse Core Ops, SparseCore 0:
  10.7 46.8 all-gather.4
  59.2 63.3 all-gather.2
  186.6 78.7 reduce-scatter.1
where the time goes:
time: 273 us; the launch traced here: 272 us
  waiting for transfers between devices  163 us (60%)
  local copies, waits for them, and re-layouts  51.4 us (19%)
  matrix products  31.5 us (12%)
  between operations  15.1 us (6%)
  blocking collectives  6.44 us (2%)
  other arithmetic  4.04 us (1%)
    reduce_scatter x1, waiting for transfers between devices, on_device(): lax.psum_scatter((grad_term * live_mask.astype(jnp.float32)[:, None, None...  76 us
    all_gather x1, waiting for transfers between devices, on_device(): lax.all_gather(weight_slots, 'dp', axis=1, tiled=True)[0]  51.8 us
    all_gather x1, waiting for transfers between devices, on_device(): whole_grad = lax.all_gather(grad_out, 'pipe', axis=1, tiled=True)  34.8 us
    transpose x1, local copies, waits for them, and re-layouts, on_device(): jnp.einsum('tkd,khd->tkh', gradient_fragments, masked, preferred_element_...  13.7 us
    dot_general x1, matrix products, on_device(): jnp.einsum('tkd,khd->tkh', gradient_fragments, masked, preferred_element_...  12.9 us
    gather x1, local copies, waits for them, and re-layouts, on_device(): gradient_fragments = grad_blocks[:, col_ids, :]  11.1 us
    dot_general x1, matrix products, on_device(): jnp.einsum('tkh,tkd->khd', act_pieces, gradient_fragments, preferred_elem...  11.1 us
    gather x1, local copies, waits for them, and re-layouts, on_device(): act_pieces = act_blocks[:, row_ids, :]  10.5 us
  transfers between devices with their start and end apart: 3, of which 3 were waited for; matrix products, arithmetic and copies ran while one was open for 7% of the time, Pallas kernels for 0%

commit v1 on v0

--- a/solution.py
+++ b/solution.py
@@ -18,7 +18,23 @@
     tok_rows = pre.shape[0]
     slab_rows = pre.shape[1] // BLOCK
     slot_cap = weight_slots.shape[1]
-    whole_grad = lax.all_gather(grad_out, "pipe", axis=1, tiled=True)
+    ways, here, hop = (lax.axis_size("pipe"), lax.axis_index("pipe"), grad_out.shape[1])
+    lengths = [n * ways if d == 1 else n for d, n in enumerate(grad_out.shape)]
+    full = lax.dynamic_update_slice_in_dim(
+        jnp.zeros(lengths, grad_out.dtype), grad_out, here * hop, axis=1
+    )
+    going_up = going_down = grad_out
+    for far in range(1, ways // 2 + 1):
+        going_up = lax.ppermute(going_up, "pipe", [(d, (d + 1) % ways) for d in range(ways)])
+        full = lax.dynamic_update_slice_in_dim(full, going_up, (here - far) % ways * hop, axis=1)
+        if 2 * far < ways:
+            going_down = lax.ppermute(
+                going_down, "pipe", [(d, (d - 1) % ways) for d in range(ways)]
+            )
+            full = lax.dynamic_update_slice_in_dim(
+                full, going_down, (here + far) % ways * hop, axis=1
+            )
+    whole_grad = full
     grad_blocks = whole_grad.reshape(tok_rows, -1, BLOCK)
     pre_wide = pre.astype(jnp.float32)
     activation, slopes = gelu_parts(pre_wide)

time: 273 us -> 227 us (0.83)
  waiting for transfers between devices: 163 us -> 102 us
  starting transfers between devices: 0.12 us -> 18.7 us
    all_gather x1, waiting for transfers between devices: 51.8 us -> 12.6 us  [on_device(): lax.all_gather(weight_slots, 'dp', axis=1, tiled=True)[0]]
    all_gather x1 -> x0, waiting for transfers between devices: 34.8 us -> none  [on_device(): whole_grad = lax.all_gather(grad_out, 'pipe', axis=1, tiled=True)]
    ppermute x0 -> x7, starting transfers between devices: none -> 18.7 us  [the longest x3 11.4 us: on_device(): lax.ppermute(going_down, 'pipe', [(d, (d - 1) % ways) for d in range(ways)])]
    ppermute x0 -> x7, waiting for transfers between devices: none -> 12.7 us  [the longest x4 12.7 us: on_device(): lax.ppermute(going_up, 'pipe', [(d, (d + 1) % ways) for d in range(ways)])]
    unnamed x14 -> x18, local copies, waits for them, and re-layouts: 9.78 us -> 9.04 us
  transfers between devices with their start and end apart: 3 -> 9, of which waited for: 3 -> 5; matrix products, arithmetic and copies ran while one was open for 7% -> 9% of each run, Pallas kernels for 0% -> 0%
where the time goes in v1:
time: 227 us
  waiting for transfers between devices  102 us (45%)
  local copies, waits for them, and re-layouts  50.2 us (22%)
  matrix products  31.4 us (14%)
  starting transfers between devices  18.7 us (8%)
  between operations  15.5 us (7%)
  blocking collectives  5.06 us (2%)
  other arithmetic  4.02 us (2%)
    reduce_scatter x1, waiting for transfers between devices, on_device(): lax.psum_scatter((grad_term * live_mask.astype(jnp.float32)[:, None, None...  75.8 us
    transpose x1, local copies, waits for them, and re-layouts, on_device(): jnp.einsum('tkd,khd->tkh', gradient_fragments, masked, preferred_element_...  13.5 us
    dot_general x1, matrix products, on_device(): jnp.einsum('tkd,khd->tkh', gradient_fragments, masked, preferred_element_...  12.9 us
    ppermute x4, waiting for transfers between devices, on_device(): lax.ppermute(going_up, 'pipe', [(d, (d + 1) % ways) for d in range(ways)])  12.7 us
    all_gather x1, waiting for transfers between devices, on_device(): lax.all_gather(weight_slots, 'dp', axis=1, tiled=True)[0]  12.6 us
    ppermute x3, starting transfers between devices, on_device(): lax.ppermute(going_down, 'pipe', [(d, (d - 1) % ways) for d in range(ways)])  11.4 us
    dot_general x1, matrix products, on_device(): jnp.einsum('tkh,tkd->khd', act_pieces, gradient_fragments, preferred_elem...  11.1 us
    gather x1, local copies, waits for them, and re-layouts, on_device(): act_pieces = act_blocks[:, row_ids, :]  10.5 us
  transfers between devices with their start and end apart: 9, of which 5 were waited for; matrix products, arithmetic and copies ran while one was open for 9% of the time, Pallas kernels for 0%

profile of v1, /device:TPU:0, one launch (start us, length us, event | category | flops | bytes accessed | tf_op | source)
XLA Modules:
  0.0 226.7 jit_solution(3703165426229686573)
XLA Ops:
  7.2 0.7 all-gather.2.cloned.1.call-update
  8.0 1.1 copy.20
  9.0 3.0 %collective-permute-start = (bf16[128,768]{0,1:T(8,128)(2,1)S(1)}, bf16[128,768]{0,1:T(8,128)(2,1)}, u32[]{:S(2)}, u32[]{:S(2)}) collective-permute-start(bf16[128,768]{0,1:T(8,128)(2,1)S(1)} %copy.20), channel_id=1, source_target_pairs={{0,1},{1,2},{2,3},{3,4},{4,5},{5,6},{6,7},{7,0},{8,9},{9,10},{10,1... | collective-permute-start | bytes 589832 | tf_op jit(solution)/shard_map/ppermute | solution.py:28
  12.1 3.1 %collective-permute-start.1 = (bf16[128,768]{0,1:T(8,128)(2,1)S(1)}, bf16[128,768]{0,1:T(8,128)(2,1)S(1)}, u32[]{:S(2)}, u32[]{:S(2)}) collective-permute-start(bf16[128,768]{0,1:T(8,128)(2,1)S(1)} %copy.20), channel_id=1, source_target_pairs={{0,7},{1,0},{2,1},{3,2},{4,3},{5,4},{6,5},{7,6},{8,15},{9,8},{10,9... | collective-permute-start | bytes 589832 | tf_op jit(solution)/shard_map/ppermute | solution.py:31
  15.8 1.2 dynamic-slice
  17.8 0.7 bitcast_dynamic-update-slice_fusion.1
  18.5 0.8 bitcast_dynamic-update-slice_fusion
  19.2 0.7 bitcast_dynamic-update-slice_fusion.2
  20.0 5.1 %all-reduce.3 = (s32[292]{0:T(512)S(1)}, s32[4]{0:T(128)S(1)}, s32[292]{0:T(512)S(1)}) all-reduce(s32[292]{0:T(512)S(1)} %bitcast_dynamic-update-slice_fusion, s32[4]{0:T(128)S(1)} %bitcast_dynamic-update-slice_fusion.1, s32[292]{0:T(512)S(1)} %bitcast_dynamic-update-slice_fusion.2), channel_id=1, replica_groups=mesh['dp'=4,'pipe'=8] {'dp'}, use_global_device_ids=true, to_apply=%add.2 | all-reduce | flops 588 | bytes 4704
  25.2 1.6 copy.25
  27.2 4.7 %collective-permute-start.3 = (bf16[128,768]{0,1:T(8,128)(2,1)S(1)}, bf16[128,768]{0,1:T(8,128)(2,1)S(1)}, u32[]{:S(2)}, u32[]{:S(2)}) collective-permute-start(bf16[128,768]{0,1:T(8,128)(2,1)S(1)} %collective-permute-done.1), channel_id=1, source_target_pairs={{0,7},{1,0},{2,1},{3,2},{4,3},{5,4},{6,5},{7,6},{8,15},{9,8},{10,9... | collective-permute-start | bytes 589832 | tf_op jit(solution)/shard_map/ppermute | solution.py:31
  31.9 1.0 constant_dynamic-update-slice_fusion.6
  32.9 3.3 %collective-permute-done.2 = bf16[128,768]{0,1:T(8,128)(2,1)S(1)} collective-permute-done((bf16[128,768]{0,1:T(8,128)(2,1)}, bf16[128,768]{0,1:T(8,128)(2,1)S(1)}, u32[]{:S(2)}, u32[]{:S(2)}) %collective-permute-start.2) | collective-permute-done | bytes 196640 | tf_op jit(solution)/shard_map/ppermute | solution.py:28
  36.2 1.7 collective-permute-start.4
  37.9 3.6 %collective-permute-start.5 = (bf16[128,768]{0,1:T(8,128)(2,1)S(1)}, bf16[128,768]{0,1:T(8,128)(2,1)S(1)}, u32[]{:S(2)}, u32[]{:S(2)}) collective-permute-start(bf16[128,768]{0,1:T(8,128)(2,1)S(1)} %collective-permute-done.3), channel_id=1, source_target_pairs={{0,7},{1,0},{2,1},{3,2},{4,3},{5,4},{6,5},{7,6},{8,15},{9,8},{10,9... | collective-permute-start | bytes 589832 | tf_op jit(solution)/shard_map/ppermute | solution.py:31
  41.5 3.6 %collective-permute-done.4 = bf16[128,768]{0,1:T(8,128)(2,1)S(1)} collective-permute-done((bf16[128,768]{0,1:T(8,128)(2,1)S(1)}, bf16[128,768]{0,1:T(8,128)(2,1)S(1)}, u32[]{:S(2)}, u32[]{:S(2)}) %collective-permute-start.4) | collective-permute-done | bytes 196640 | tf_op jit(solution)/shard_map/ppermute | solution.py:28
  45.1 2.5 %collective-permute-start.6 = (bf16[128,768]{0,1:T(8,128)(2,1)S(1)}, bf16[128,768]{0,1:T(8,128)(2,1)S(1)}, u32[]{:S(2)}, u32[]{:S(2)}) collective-permute-start(bf16[128,768]{0,1:T(8,128)(2,1)S(1)} %collective-permute-done.4), channel_id=1, source_target_pairs={{0,1},{1,2},{2,3},{3,4},{4,5},{5,6},{6,7},{7,0},{8,9},{9,10},{10,1... | collective-permute-start | bytes 589832 | tf_op jit(solution)/shard_map/ppermute | solution.py:28
  47.7 5.8 %collective-permute-done.6 = bf16[128,768]{0,1:T(8,128)(2,1)S(1)} collective-permute-done((bf16[128,768]{0,1:T(8,128)(2,1)S(1)}, bf16[128,768]{0,1:T(8,128)(2,1)S(1)}, u32[]{:S(2)}, u32[]{:S(2)}) %collective-permute-start.6) | collective-permute-done | bytes 196640 | tf_op jit(solution)/shard_map/ppermute | solution.py:28
  53.5 0.9 copy.23
  54.4 10.5 %gather_fusion = bf16[292,128,128]{2,1,0:T(8,128)(2,1)} fusion(bf16[128,48,128]{2,0,1:T(8,128)(2,1)S(1)} %copy.23, s32[1024]{0:T(1024)S(1)} %pad_clamp_fusion.1), kind=kCustom, calls=%fused_computation | custom fusion | bytes 19137680 | tf_op jit(solution)/shard_map/gather | solution.py:53
  64.9 12.6 %all-gather.2.cloned.1.call-done = bf16[1,292,128,128]{3,2,0,1:T(8,128)(2,1)} async-done(((bf16[1,73,128,128]{3,2,0,1:T(8,128)(2,1)}), bf16[1,292,128,128]{3,2,0,1:T(8,128)(2,1)}) %all-gather.2.cloned.1.call-update) | async-done | bytes 9568272 | tf_op jit(solution)/shard_map/all_gather | solution.py:55
  77.4 12.9 %fusion.5 = bf16[128,292,128]{0,2,1:T(8,128)(2,1)} fusion(bf16[292,128,128]{2,1,0:T(8,128)(2,1)} %gather_fusion, bf16[1,292,128,128]{3,2,0,1:T(8,128)(2,1)} %all-gather.2.cloned.1.call-done, bf16[292]{0:T(512)(128)(2,1)S(1)} %convert_element_type.27), kind=kOutput, calls=%fused_computation.9 | convolution fusion | flops 1229520896 | bytes 28705352 | tf_op jit(solution)/shard_map/tkd,khd->tkh/dot_general | solution.py:58
  90.3 13.5 %copy.24 = bf16[128,292,128]{2,1,0:T(8,128)(2,1)} copy(bf16[128,292,128]{0,2,1:T(8,128)(2,1)} %fusion.5) | data formatting | bytes 19136512 | tf_op jit(solution)/shard_map/tkd,khd->tkh/transpose | solution.py:58
  103.9 7.4 %convolution_bitcast_fusion = f32[128,48,128]{2,1,0:T(8,128)} fusion(bf16[128,292,128]{2,1,0:T(8,128)(2,1)} %copy.24, s32[292]{0:T(512)S(1)} %copy-done.3), kind=kOutput, calls=%fused_computation.25 | convolution fusion | flops 459290304 | bytes 12715152 | tf_op jit(solution)/shard_map/tkh,kr->trh/dot_general | solution.py:62
  111.3 2.4 %copy.31 = f32[128,48,128]{0,2,1:T(8,128)S(1)} copy(f32[128,48,128]{2,1,0:T(8,128)} %convolution_bitcast_fusion) | data formatting | bytes 6291456 | tf_op jit(solution)/shard_map/reshape | solution.py:78
  113.7 3.9 %fusion.21 = (bf16[128,6144]{0,1:T(8,128)(2,1)}, bf16[128,6144]{0,1:T(8,128)(2,1)}) fusion(bf16[128,6144]{0,1:T(8,128)(2,1)} %copy.25, f32[128,48,128]{0,2,1:T(8,128)S(1)} %copy.31), kind=kLoop, calls=%fused_computation.24 | loop fusion | flops 10223616 | bytes 7864320 | tf_op jit(solution)/shard_map/convert_element_type | solution.py:41
  117.7 1.9 copy.27
  119.6 10.5 %gather_fusion.1 = bf16[292,128,128]{2,1,0:T(8,128)(2,1)} fusion(bf16[128,48,128]{2,0,1:T(8,128)(2,1)S(1)} %copy.27, s32[1024]{0:T(1024)S(1)} %pad_clamp_fusion), kind=kCustom, calls=%fused_computation.1 | custom fusion | bytes 19137680 | tf_op jit(solution)/shard_map/gather | solution.py:66
  130.0 11.1 %multiply_convert_fusion = bf16[292,128,128]{2,1,0:T(8,128)(2,1)} fusion(f32[292]{0:T(512)S(1)} %get-tuple-element.9, bf16[292,128,128]{2,1,0:T(8,128)(2,1)} %gather_fusion, bf16[292,128,128]{2,1,0:T(8,128)(2,1)} %gather_fusion.1), kind=kOutput, calls=%fused_computation.2 | convolution fusion | flops 1234305024 | bytes 28705936 | tf_op jit(solution)/shard_map/tkh,tkd->khd/dot_general | solution.py:68
  141.1 1.4 copy-done
  142.5 1.6 copy.29
  144.1 75.8 %reduce-scatter.2.cloned.1.call-done = bf16[73,128,128]{2,1,0:T(8,128)(2,1)} async-done(((bf16[292,128,128]{2,1,0:T(8,128)(2,1)}), bf16[73,128,128]{2,1,0:T(8,128)(2,1)}) %reduce-scatter.2.cloned.1.call-update) | async-done | bytes 2392080 | tf_op jit(solution)/shard_map/reduce_scatter | solution.py:71
  (34 shorter events, 0.8 us)
Async XLA Ops:
  7.2 18.0 %copy-start.1 = (bf16[128,6144]{1,0:T(8,128)(2,1)S(1)}, bf16[128,6144]{1,0:T(8,128)(2,1)}, u32[]{:S(2)}) copy-start(bf16[128,6144]{1,0:T(8,128)(2,1)} %param.6) | copy-start | bytes 4718596
  7.2 70.3 %all-gather.2.cloned.1.call-start = ((), (), s32[]{:S(2)}) async-start(), calls=%async_computation.1 | async-start | bytes 11960320 | tf_op jit(solution)/shard_map/all_gather | solution.py:55
  7.9 212.0 %reduce-scatter.2.cloned.1.call-start = ((), (), s32[]{:S(2)}) async-start(), calls=%async_computation.2 | async-start | bytes 11960320 | tf_op jit(solution)/shard_map/reduce_scatter | solution.py:71
  9.0 18.1 %collective-permute-start = (bf16[128,768]{0,1:T(8,128)(2,1)S(1)}, bf16[128,768]{0,1:T(8,128)(2,1)}, u32[]{:S(2)}, u32[]{:S(2)}) collective-permute-start(bf16[128,768]{0,1:T(8,128)(2,1)S(1)} %copy.20), channel_id=1, source_target_pairs={{0,1},{1,2},{2,3},{3,4},{4,5},{5,6},{6,7},{7,0},{8,9},{9,10},{10,1... | collective-permute-start | bytes 589832 | tf_op jit(solution)/shard_map/ppermute | solution.py:28
  12.1 15.1 %collective-permute-start.1 = (bf16[128,768]{0,1:T(8,128)(2,1)S(1)}, bf16[128,768]{0,1:T(8,128)(2,1)S(1)}, u32[]{:S(2)}, u32[]{:S(2)}) collective-permute-start(bf16[128,768]{0,1:T(8,128)(2,1)S(1)} %copy.20), channel_id=1, source_target_pairs={{0,7},{1,0},{2,1},{3,2},{4,3},{5,4},{6,5},{7,6},{8,15},{9,8},{10,9... | collective-permute-start | bytes 589832 | tf_op jit(solution)/shard_map/ppermute | solution.py:31
  25.0 1.8 copy-start.2
  27.1 9.0 %collective-permute-start.2 = (bf16[128,768]{0,1:T(8,128)(2,1)}, bf16[128,768]{0,1:T(8,128)(2,1)S(1)}, u32[]{:S(2)}, u32[]{:S(2)}) collective-permute-start(bf16[128,768]{0,1:T(8,128)(2,1)} %collective-permute-done), channel_id=1, source_target_pairs={{0,1},{1,2},{2,3},{3,4},{4,5},{5,6},{6,7},{7,0},{8,9},{9,10},{10,1... | collective-permute-start | bytes 589832 | tf_op jit(solution)/shard_map/ppermute | solution.py:28
  27.2 10.7 %collective-permute-start.3 = (bf16[128,768]{0,1:T(8,128)(2,1)S(1)}, bf16[128,768]{0,1:T(8,128)(2,1)S(1)}, u32[]{:S(2)}, u32[]{:S(2)}) collective-permute-start(bf16[128,768]{0,1:T(8,128)(2,1)S(1)} %collective-permute-done.1), channel_id=1, source_target_pairs={{0,7},{1,0},{2,1},{3,2},{4,3},{5,4},{6,5},{7,6},{8,15},{9,8},{10,9... | collective-permute-start | bytes 589832 | tf_op jit(solution)/shard_map/ppermute | solution.py:31
  36.2 8.9 %collective-permute-start.4 = (bf16[128,768]{0,1:T(8,128)(2,1)S(1)}, bf16[128,768]{0,1:T(8,128)(2,1)S(1)}, u32[]{:S(2)}, u32[]{:S(2)}) collective-permute-start(bf16[128,768]{0,1:T(8,128)(2,1)S(1)} %collective-permute-done.2), channel_id=1, source_target_pairs={{0,1},{1,2},{2,3},{3,4},{4,5},{5,6},{6,7},{7,0},{8,9},{9,10},{10,1... | collective-permute-start | bytes 589832 | tf_op jit(solution)/shard_map/ppermute | solution.py:28
  37.9 9.8 %collective-permute-start.5 = (bf16[128,768]{0,1:T(8,128)(2,1)S(1)}, bf16[128,768]{0,1:T(8,128)(2,1)S(1)}, u32[]{:S(2)}, u32[]{:S(2)}) collective-permute-start(bf16[128,768]{0,1:T(8,128)(2,1)S(1)} %collective-permute-done.3), channel_id=1, source_target_pairs={{0,7},{1,0},{2,1},{3,2},{4,3},{5,4},{6,5},{7,6},{8,15},{9,8},{10,9... | collective-permute-start | bytes 589832 | tf_op jit(solution)/shard_map/ppermute | solution.py:31
  45.1 8.4 %collective-permute-start.6 = (bf16[128,768]{0,1:T(8,128)(2,1)S(1)}, bf16[128,768]{0,1:T(8,128)(2,1)S(1)}, u32[]{:S(2)}, u32[]{:S(2)}) collective-permute-start(bf16[128,768]{0,1:T(8,128)(2,1)S(1)} %collective-permute-done.4), channel_id=1, source_target_pairs={{0,1},{1,2},{2,3},{3,4},{4,5},{5,6},{6,7},{7,0},{8,9},{9,10},{10,1... | collective-permute-start | bytes 589832 | tf_op jit(solution)/shard_map/ppermute | solution.py:28
  90.3 13.5 %copy-start.3 = (s32[292]{0:T(512)S(1)}, s32[292]{0:T(512)}, u32[]{:S(2)}) copy-start(s32[292]{0:T(512)} %copy-done.2) | copy-start | bytes 3508
  141.1 1.4 copy-start
Sparse Core Ops, SparseCore 0:
  9.5 67.8 all-gather.1
  141.3 78.5 reduce-scatter.1
